TPU v7x, 32 devices: a whole 2x2x4 slice. The times are simulated.
32 devices in a mesh: dp: 8 (over z, x), tensor: 4 (over y, core).
Axes of the slice: x: 2, y: 2, z: 4, core: 2. Of those that a mesh axis runs over, the one named last changes fastest.
Arguments:
- tokens: bfloat16 [4096, 4096], P(('dp', 'tensor')), may hold values from -6 to 6
- norm_gain: float32 [4096], replicated, may hold values from 0.1 to 1.9
- w_query: bfloat16 [4096, 2048], P(None, 'tensor'), may hold values from -2 to 2
- key_weight: bfloat16 [4096, 512], P(None, 'tensor'), may hold values from -0.09375 to 0.09375
- value_weight: bfloat16 [4096, 512], P(None, 'tensor'), may hold values from -0.09375 to 0.09375
- w_out: bfloat16 [2048, 4096], P('tensor'), may hold values from -0.125 to 0.125
- lengths: int32 [4], replicated, may hold values from 1 to 2560, 4096 in all
Outputs:
- layer_out: bfloat16 [4096, 4096], P(('dp', 'tensor'))
Inputs may be any that keep to these rules, and one draw needn't show every extreme that they name: The lengths sum to 4096, and some document has exactly 2560 tokens.
All inputs are finite; a program needn't handle non-finite values.
Results may differ from a plain program's by a relative error of at most 0.0095.
The roundings to bfloat16 on the way count: a program that leaves them out, or rounds other values in their place, can miss the bound.
Values may be sent and summed in bfloat16 or wider, within the bound.
A program may use at most 128 MiB of HBM per device.

v0:
```python
import jax
import jax.numpy as jnp
from jax import lax
from jax.sharding import PartitionSpec as P

HEAD_SIZE = 128
epsilon = 1e-05
rope_base = 500000.0
masked = -1e30
initial_peak = -1e29


def from_behind(block, axis, distance):
    devices = range(lax.axis_size(axis))
    route = [(i - distance, i) for i in devices if i - distance in devices]
    return lax.ppermute(block, axis, route)


def doc_starts(lengths, positions):
    doc_ends = jnp.cumsum(lengths)
    closed = (doc_ends[None, :] <= positions[:, None]).astype(jnp.int32)
    return jnp.sum(closed * lengths[None, :], axis=1)


def rotate(vectors, offsets):
    half_width = vectors.shape[-1] // 2
    exponent = jnp.arange(half_width, dtype=jnp.float32) * (-2.0 / vectors.shape[-1])
    frequency = rope_base**exponent
    angles = offsets.astype(jnp.float32)[:, None] * frequency[None, :]
    cos_part = jnp.cos(angles)[:, None, :]
    sin_part = jnp.sin(angles)[:, None, :]
    leading = vectors[..., :half_width]
    trailing = vectors[..., half_width:]
    return jnp.concatenate(
        [leading * cos_part - trailing * sin_part, trailing * cos_part + leading * sin_part],
        axis=-1,
    )


def project(tokens, norm_gain, w_query, key_weight, value_weight, positions, starts):
    count = tokens.shape[0]
    wide = tokens.astype(jnp.float32)
    inverse = lax.rsqrt(jnp.mean(wide * wide, axis=1, keepdims=True) + epsilon)
    normed = (wide * inverse * norm_gain[None, :]).astype(jnp.bfloat16)
    offsets = positions - starts
    query_rows = jnp.dot(normed, w_query, preferred_element_type=jnp.float32).reshape(
        count, -1, HEAD_SIZE
    )
    query_rows = rotate(query_rows, offsets).astype(jnp.bfloat16)
    key = jnp.dot(normed, key_weight, preferred_element_type=jnp.float32).reshape(
        count, -1, HEAD_SIZE
    )
    key = rotate(key, offsets).astype(jnp.bfloat16)
    value_rows = jnp.dot(normed, value_weight, preferred_element_type=jnp.float32).astype(
        jnp.bfloat16
    )
    return (query_rows, key.reshape(count, -1), value_rows)


def attend_block(carry, keys, values, first_key, context):
    query_rows, positions, starts = context
    length = keys.shape[0]
    heads = query_rows.shape[1]
    key_pos = first_key + jnp.arange(length, dtype=jnp.int32)
    useful = (first_key + length - 1 >= starts[0]) & (first_key <= positions[-1])
    scale = query_rows.shape[-1] ** (-0.5)

    def compute(state):
        peak, mass, summed = state
        key_view = keys.reshape(length, heads, -1)
        value_view = values.reshape(length, heads, -1)
        scores = (
            jnp.einsum("qkgd,skd->qkgs", query_rows, key_view, preferred_element_type=jnp.float32)
            * scale
        )
        visible = (key_pos[None, :] >= starts[:, None]) & (key_pos[None, :] <= positions[:, None])
        scores = jnp.where(visible[:, None, None, :], scores, masked)
        fresh = jnp.maximum(peak, jnp.max(scores, axis=-1))
        shrink = jnp.exp(peak - fresh)
        probs = jnp.exp(scores - fresh[..., None])
        mass = mass * shrink + jnp.sum(probs, axis=-1)
        update = jnp.einsum(
            "qkgs,skd->qkgd",
            probs.astype(jnp.bfloat16),
            value_view,
            preferred_element_type=jnp.float32,
        )
        summed = summed * shrink[..., None] + update
        return (fresh, mass, summed)

    def unchanged(state):
        return state

    return lax.cond(useful, compute, unchanged, carry)


def fold_keys(carry, pieces, start, context):
    keys, values = pieces
    width = keys.shape[0]
    size = min(width, 1024)
    whole = width // size

    def one_block(index, state):
        offset = (index * size).astype(jnp.int32)
        return attend_block(state, keys, values, start + offset, context)

    carry = lax.fori_loop(0, whole, one_block, carry)
    return carry


def body(tokens, norm_gain, w_query, key_weight, value_weight, w_out, lengths):
    gathered = lax.all_gather(tokens, "tensor", axis=0, tiled=True)
    count = gathered.shape[0]
    first = lax.axis_index("dp") * count
    positions = first + jnp.arange(count, dtype=jnp.int32)
    starts = doc_starts(lengths, positions)
    query_rows, key, value_rows = project(
        gathered, norm_gain, w_query, key_weight, value_weight, positions, starts
    )
    heads = key.shape[1] // HEAD_SIZE
    query_rows = query_rows.reshape(count, heads, -1, HEAD_SIZE)
    group_count = query_rows.shape[2]
    context = (query_rows, positions, starts)
    initial = (
        jnp.full((count, heads, group_count), initial_peak, jnp.float32),
        jnp.zeros((count, heads, group_count), jnp.float32),
        jnp.zeros((count, heads, group_count, HEAD_SIZE), jnp.float32),
    )
    carry = fold_keys(initial, (key, value_rows), first, context)
    paired = jnp.stack([key, value_rows])
    reach = lax.axis_size("dp") // 2 + 1

    def one_step(back, state):
        moving, accum = state
        moving = from_behind(moving, "dp", 1)
        accum = fold_keys(accum, (moving[0], moving[1]), first - back * count, context)
        return (moving, accum)

    paired, carry = lax.fori_loop(1, reach + 1, one_step, (paired, carry))
    peak, mass, summed = carry
    attended = (summed / mass[..., None]).reshape(count, -1).astype(jnp.bfloat16)
    branch = lax.psum_scatter(
        jnp.dot(attended, w_out, preferred_element_type=jnp.float32).astype(jnp.bfloat16),
        "tensor",
        scatter_dimension=0,
        tiled=True,
    ).astype(jnp.float32)
    return (tokens.astype(jnp.float32) + branch).astype(jnp.bfloat16)


def solution(mesh):
    in_specs = (
        P(("dp", "tensor"), None),
        P(),
        P(None, "tensor"),
        P(None, "tensor"),
        P(None, "tensor"),
        P("tensor", None),
        P(),
    )
    out_specs = P(("dp", "tensor"), None)
    return jax.shard_map(body, mesh=mesh, in_specs=in_specs, out_specs=out_specs, check_vma=False)
```

profile of v0, /device:TPU:0, one launch (start us, length us, event | category | flops | bytes accessed | tf_op | source)
XLA Modules:
  0.0 201.6 jit_solution(4432884227593100175)
XLA Ops:
  6.5 0.7 all-gather.2.cloned.1.call-update
  7.3 0.7 slice.69
  8.0 0.8 reduce-window.8
  8.8 0.7 select_reduce_fusion
  9.6 0.5 slice.68
  11.5 1.0 broadcast_in_dim.24
  12.5 1.8 multiply_cosine_fusion
  14.3 31.8 %all-gather.2.cloned.1.call-done = bf16[512,4096]{1,0:T(8,128)(2,1)} async-done(((bf16[128,4096]{1,0:T(8,128)(2,1)}), bf16[512,4096]{1,0:T(8,128)(2,1)}) %all-gather.2.cloned.1.call-update) | async-done | bytes 4194320 | tf_op jit(solution)/shard_map/all_gather | solution.py:112
  46.1 3.2 %fusion.42 = f32[512]{0:T(512)S(1)} fusion(bf16[512,4096]{1,0:T(8,128)(2,1)} %all-gather.2.cloned.1.call-done), kind=kLoop, calls=%fused_computation.47 | loop fusion | flops 6290944 | bytes 4196352 | tf_op jit(solution)/shard_map/reduce_sum | solution.py:43
  49.6 1.6 convolution_bitcast_fusion
  51.2 0.6 fusion.52
  51.8 1.6 convolution_convert_fusion.1
  53.5 0.8 copy.32
  54.3 5.9 %fusion.55 = f32[512,512]{0,1:T(8,128)S(1)} fusion(bf16[4096,512]{1,0:T(8,128)(2,1)} %param.15, bf16[512,4096]{1,0:T(8,128)(2,1)} %all-gather.2.cloned.1.call-done, f32[4096]{0:T(1024)S(1)} %copy-done.13, f32[512]{0:T(512)S(1)} %add_rsqrt_fusion), kind=kOutput, calls=%fused_computation.79 | convolution fusion | flops 2155872256 | bytes 9455616 | tf_op jit(solution)/shard_map/dot_general | solution.py:46
  60.2 0.9 fusion.59
  61.1 0.3 copy.40
  61.5 1.4 copy.39
  62.9 1.2 fusion.45
  64.1 0.3 pad_maximum_fusion
  64.4 5.8 %conditional.2 = ((f32[512,1,4]{0,2,1:T(4,128)S(1)}, f32[512,1,4]{0,2,1:T(4,128)S(1)}, f32[512,1,4,128]{3,0,2,1:T(8,128)})) conditional(s32[]{:T(128)} %convert_element_type.89, (f32[512,1,4]{0,2,1:T(4,128)S(1)}, f32[512,1,4]{0,2,1:T(4,128)S(1)}, f32[512,1,4,128]{3,0,2,1:T(8,128)}) %tuple.55, (s32[512]{0:T(512)}, s32[512]{0:T(512)}, ...), branch_computations={%region_3.4_spmd, %region_4.7_spmd} | conditional | flops 549722112 | bytes 25563252 | solution.py:94
  64.6 1.0 compare_and_fusion
  65.7 0.9 fusion.2
  66.6 0.9 fusion.1
  67.6 1.6 fusion.10
  69.2 1.0 copy-done.4
  70.2 56.5 %while.45 = (s32[]{:T(128)}, bf16[2,512,128]{2,1,0:T(8,128)(2,1)S(1)}, f32[512,1,4]{0,2,1:T(4,128)S(1)}, f32[512,1,4]{0,2,1:T(4,128)S(1)}, f32[512,1,4,128]{3,0,...) while((s32[]{:T(128)}, ...), condition=%wide.region_12.13_spmd, body=%wide.region_7.12_spmd.sunk | while | flops 549722624 | bytes 26620328 | solution.py:139
  70.2 3.4 %collective-permute-start = (bf16[2,512,128]{2,1,0:T(8,128)(2,1)S(1)}, bf16[2,512,128]{2,1,0:T(8,128)(2,1)S(1)}, u32[]{:S(2)}, u32[]{:S(2)}) collective-permute-start(bf16[2,512,128]{2,1,0:T(8,128)(2,1)S(1)} %get-tuple-element.655), channel_id=1, source_target_pairs={{0,4},{4,8},{8,12},{12,16},{16,20},{20,24},{24,28},{1,5},{5,9},{9,... | collective-permute-start | bytes 786440 | tf_op jit(solution)/shard_map/while/body/eval_jaxpr/ppermute | solution.py:16
  73.6 1.2 slice.94
  74.8 1.3 slice.95
  77.2 2.3 %collective-permute-done = bf16[2,512,128]{2,1,0:T(8,128)(2,1)S(1)} collective-permute-done((bf16[2,512,128]{2,1,0:T(8,128)(2,1)S(1)}, bf16[2,512,128]{2,1,0:T(8,128)(2,1)S(1)}, u32[]{:S(2)}, u32[]{:S(2)}) %collective-permute-start) | collective-permute-done | bytes 262176 | tf_op jit(solution)/shard_map/while/body/eval_jaxpr/ppermute | solution.py:16
  79.6 9.7 %collective-permute-start = (bf16[2,512,128]{2,1,0:T(8,128)(2,1)S(1)}, bf16[2,512,128]{2,1,0:T(8,128)(2,1)S(1)}, u32[]{:S(2)}, u32[]{:S(2)}) collective-permute-start(bf16[2,512,128]{2,1,0:T(8,128)(2,1)S(1)} %get-tuple-element.655), channel_id=1, source_target_pairs={{0,4},{4,8},{8,12},{12,16},{16,20},{20,24},{24,28},{1,5},{5,9},{9,... | collective-permute-start | bytes 786440 | tf_op jit(solution)/shard_map/while/body/eval_jaxpr/ppermute | solution.py:16
  89.3 1.2 slice.94
  90.5 1.3 slice.95
  92.9 1.4 collective-permute-done
  94.4 4.4 %collective-permute-start = (bf16[2,512,128]{2,1,0:T(8,128)(2,1)S(1)}, bf16[2,512,128]{2,1,0:T(8,128)(2,1)S(1)}, u32[]{:S(2)}, u32[]{:S(2)}) collective-permute-start(bf16[2,512,128]{2,1,0:T(8,128)(2,1)S(1)} %get-tuple-element.655), channel_id=1, source_target_pairs={{0,4},{4,8},{8,12},{12,16},{16,20},{20,24},{24,28},{1,5},{5,9},{9,... | collective-permute-start | bytes 786440 | tf_op jit(solution)/shard_map/while/body/eval_jaxpr/ppermute | solution.py:16
  98.8 1.2 slice.94
  100.0 1.3 slice.95
  102.5 0.6 collective-permute-done
  103.1 10.5 %collective-permute-start = (bf16[2,512,128]{2,1,0:T(8,128)(2,1)S(1)}, bf16[2,512,128]{2,1,0:T(8,128)(2,1)S(1)}, u32[]{:S(2)}, u32[]{:S(2)}) collective-permute-start(bf16[2,512,128]{2,1,0:T(8,128)(2,1)S(1)} %get-tuple-element.655), channel_id=1, source_target_pairs={{0,4},{4,8},{8,12},{12,16},{16,20},{20,24},{24,28},{1,5},{5,9},{9,... | collective-permute-start | bytes 786440 | tf_op jit(solution)/shard_map/while/body/eval_jaxpr/ppermute | solution.py:16
  113.6 1.2 slice.94
  114.8 1.3 slice.95
  117.5 5.3 %collective-permute-start = (bf16[2,512,128]{2,1,0:T(8,128)(2,1)S(1)}, bf16[2,512,128]{2,1,0:T(8,128)(2,1)S(1)}, u32[]{:S(2)}, u32[]{:S(2)}) collective-permute-start(bf16[2,512,128]{2,1,0:T(8,128)(2,1)S(1)} %get-tuple-element.655), channel_id=1, source_target_pairs={{0,4},{4,8},{8,12},{12,16},{16,20},{20,24},{24,28},{1,5},{5,9},{9,... | collective-permute-start | bytes 786440 | tf_op jit(solution)/shard_map/while/body/eval_jaxpr/ppermute | solution.py:16
  122.8 1.2 slice.94
  124.0 1.3 slice.95
  126.7 1.6 copy.33
  128.4 6.5 %convolution_convert_fusion = bf16[512,4096]{1,0:T(8,128)(2,1)} fusion(bf16[512,512]{0,1:T(8,128)(2,1)S(1)} %bitcast.139, bf16[512,4096]{1,0:T(8,128)(2,1)} %param.18), kind=kOutput, calls=%fused_computation.50 | convolution fusion | flops 2149580800 | bytes 8912896 | tf_op jit(solution)/shard_map/dot_general | solution.py:143
  134.9 57.3 %reduce-scatter.2.cloned.1.call-done = bf16[128,4096]{1,0:T(8,128)(2,1)} async-done(((bf16[512,4096]{1,0:T(8,128)(2,1)}), bf16[128,4096]{1,0:T(8,128)(2,1)}) %reduce-scatter.2.cloned.1.call-update) | async-done | bytes 1048592 | tf_op jit(solution)/shard_map/reduce_scatter | solution.py:142
  192.3 2.4 %add_convert_fusion = bf16[128,4096]{1,0:T(8,128)(2,1)} fusion(bf16[128,4096]{1,0:T(8,128)(2,1)} %reduce-scatter.2.cloned.1.call-done, bf16[128,4096]{1,0:T(8,128)(2,1)S(1)} %copy-done.1), kind=kLoop, calls=%fused_computation.51 | loop fusion | flops 2097152 | bytes 3145728 | tf_op jit(solution)/shard_map/convert_element_type | solution.py:148
  (55 shorter events, 1.0 us)
Async XLA Ops:
  6.5 42.8 %copy-start = (bf16[4096,128]{1,0:T(8,128)(2,1)S(1)}, bf16[4096,128]{1,0:T(8,128)(2,1)}, u32[]{:S(2)}) copy-start(bf16[4096,128]{1,0:T(8,128)(2,1)} %param.16) | copy-start | bytes 3145732
  6.5 42.8 %copy-start.13 = (f32[4096]{0:T(1024)S(1)}, f32[4096]{0:T(1024)}, u32[]{:S(2)}) copy-start(f32[4096]{0:T(1024)} %param.14) | copy-start | bytes 49156
  6.5 39.6 %all-gather.2.cloned.1.call-start = ((), (), s32[]{:S(2)}) async-start(), calls=%async_computation.1 | async-start | bytes 5242880 | tf_op jit(solution)/shard_map/all_gather | solution.py:112
  7.3 185.0 %reduce-scatter.2.cloned.1.call-start = ((), (), s32[]{:S(2)}) async-start(), calls=%async_computation.2 | async-start | bytes 5242880 | tf_op jit(solution)/shard_map/reduce_scatter | solution.py:142
  7.3 43.9 %copy-start.8 = (s32[512]{0:T(512)}, s32[512]{0:T(512)S(1)}, u32[]{:S(2)}) copy-start(s32[512]{0:T(512)S(1)} %iota_add_fusion) | copy-start | bytes 6148
  9.6 2.9 %copy-start.9 = (s32[512]{0:T(512)}, s32[512]{0:T(512)S(1)}, u32[]{:S(2)}) copy-start(s32[512]{0:T(512)S(1)} %select_reduce_fusion) | copy-start | bytes 6148
  46.1 3.4 %copy-start.2 = (bf16[512,4096]{1,0:T(8,128)(2,1)S(1)}, bf16[512,4096]{1,0:T(8,128)(2,1)}, u32[]{:S(2)}) copy-start(bf16[512,4096]{1,0:T(8,128)(2,1)} %all-gather.2.cloned.1.call-done) | copy-start | bytes 12582916
  49.6 2.2 %copy-start.12 = (bf16[4096,128]{1,0:T(8,128)(2,1)S(1)}, bf16[4096,128]{1,0:T(8,128)(2,1)}, u32[]{:S(2)}) copy-start(bf16[4096,128]{1,0:T(8,128)(2,1)} %param.17) | copy-start | bytes 3145732
  53.4 6.8 %copy-start.10 = (bf16[512,128]{0,1:T(8,128)(2,1)}, bf16[512,128]{0,1:T(8,128)(2,1)S(1)}, u32[]{:S(2)}) copy-start(bf16[512,128]{0,1:T(8,128)(2,1)S(1)} %convolution_convert_fusion.1) | copy-start | bytes 393220
  64.4 5.8 %copy-start.7 = (bf16[2,512,128]{2,1,0:T(8,128)(2,1)S(1)}, bf16[2,512,128]{2,1,0:T(8,128)(2,1)}, u32[]{:S(2)}) copy-start(bf16[2,512,128]{2,1,0:T(8,128)(2,1)} %copy.32) | copy-start | bytes 786436
  65.6 1.9 copy-start.3
  65.6 1.9 copy-start.11
  69.2 1.0 copy-start.4
  70.2 9.3 %collective-permute-start = (bf16[2,512,128]{2,1,0:T(8,128)(2,1)S(1)}, bf16[2,512,128]{2,1,0:T(8,128)(2,1)S(1)}, u32[]{:S(2)}, u32[]{:S(2)}) collective-permute-start(bf16[2,512,128]{2,1,0:T(8,128)(2,1)S(1)} %get-tuple-element.655), channel_id=1, source_target_pairs={{0,4},{4,8},{8,12},{12,16},{16,20},{20,24},{24,28},{1,5},{5,9},{9,... | collective-permute-start | bytes 786440 | tf_op jit(solution)/shard_map/while/body/eval_jaxpr/ppermute | solution.py:16
  79.6 14.8 %collective-permute-start = (bf16[2,512,128]{2,1,0:T(8,128)(2,1)S(1)}, bf16[2,512,128]{2,1,0:T(8,128)(2,1)S(1)}, u32[]{:S(2)}, u32[]{:S(2)}) collective-permute-start(bf16[2,512,128]{2,1,0:T(8,128)(2,1)S(1)} %get-tuple-element.655), channel_id=1, source_target_pairs={{0,4},{4,8},{8,12},{12,16},{16,20},{20,24},{24,28},{1,5},{5,9},{9,... | collective-permute-start | bytes 786440 | tf_op jit(solution)/shard_map/while/body/eval_jaxpr/ppermute | solution.py:16
  94.4 8.6 %collective-permute-start = (bf16[2,512,128]{2,1,0:T(8,128)(2,1)S(1)}, bf16[2,512,128]{2,1,0:T(8,128)(2,1)S(1)}, u32[]{:S(2)}, u32[]{:S(2)}) collective-permute-start(bf16[2,512,128]{2,1,0:T(8,128)(2,1)S(1)} %get-tuple-element.655), channel_id=1, source_target_pairs={{0,4},{4,8},{8,12},{12,16},{16,20},{20,24},{24,28},{1,5},{5,9},{9,... | collective-permute-start | bytes 786440 | tf_op jit(solution)/shard_map/while/body/eval_jaxpr/ppermute | solution.py:16
  103.1 14.4 %collective-permute-start = (bf16[2,512,128]{2,1,0:T(8,128)(2,1)S(1)}, bf16[2,512,128]{2,1,0:T(8,128)(2,1)S(1)}, u32[]{:S(2)}, u32[]{:S(2)}) collective-permute-start(bf16[2,512,128]{2,1,0:T(8,128)(2,1)S(1)} %get-tuple-element.655), channel_id=1, source_target_pairs={{0,4},{4,8},{8,12},{12,16},{16,20},{20,24},{24,28},{1,5},{5,9},{9,... | collective-permute-start | bytes 786440 | tf_op jit(solution)/shard_map/while/body/eval_jaxpr/ppermute | solution.py:16
  117.5 9.2 %collective-permute-start = (bf16[2,512,128]{2,1,0:T(8,128)(2,1)S(1)}, bf16[2,512,128]{2,1,0:T(8,128)(2,1)S(1)}, u32[]{:S(2)}, u32[]{:S(2)}) collective-permute-start(bf16[2,512,128]{2,1,0:T(8,128)(2,1)S(1)} %get-tuple-element.655), channel_id=1, source_target_pairs={{0,4},{4,8},{8,12},{12,16},{16,20},{20,24},{24,28},{1,5},{5,9},{9,... | collective-permute-start | bytes 786440 | tf_op jit(solution)/shard_map/while/body/eval_jaxpr/ppermute | solution.py:16
  134.9 57.4 %copy-start.1 = (bf16[128,4096]{1,0:T(8,128)(2,1)S(1)}, bf16[128,4096]{1,0:T(8,128)(2,1)}, u32[]{:S(2)}) copy-start(bf16[128,4096]{1,0:T(8,128)(2,1)} %param.13) | copy-start | bytes 3145732
Sparse Core Ops, SparseCore 0:
  8.9 37.1 all-gather.1
  135.1 57.1 reduce-scatter.1
where the time goes:
time: 202 us
  waiting for transfers between devices  94.5 us (47%)
  starting transfers between devices  33.3 us (16%)
  local copies, waits for them, and re-layouts  20.8 us (10%)
  matrix products  18.3 us (9%)
  between operations  14.9 us (7%)
  other arithmetic  13.2 us (7%)
  loops' own time  6.45 us (3%)
    reduce_scatter x1, waiting for transfers between devices, body(): lax.psum_scatter(jnp.dot(attended, w_out, preferred_element_type=jnp.floa...  57.3 us
    ppermute x5, starting transfers between devices, from_behind(): return lax.ppermute(block, axis, route)  33.3 us
    all_gather x1, waiting for transfers between devices, body(): gathered = lax.all_gather(tokens, 'tensor', axis=0, tiled=True)  31.8 us
    slice x6, local copies, waits for them, and re-layouts, attend_block(): positions[-1]  7.09 us
    dot_general x1, matrix products, body(): jnp.dot(attended, w_out, preferred_element_type=jnp.float32)  6.51 us
    slice x6, local copies, waits for them, and re-layouts, attend_block(): starts[0]  6.39 us
    another operation x1, loops' own time, body(): paired, carry = lax.fori_loop(1, reach + 1, one_step, (paired, carry))  6.17 us
    dot_general x1, matrix products, project(): jnp.dot(normed, w_query, preferred_element_type=jnp.float32)  5.94 us
  transfers between devices with their start and end apart: 7, of which 7 were waited for; matrix products, arithmetic and copies ran while one was open for 9% of the time, Pallas kernels for 0%

commit v1 on v0

--- a/solution.py
+++ b/solution.py
@@ -109,7 +109,9 @@
 
 
 def body(tokens, norm_gain, w_query, key_weight, value_weight, w_out, lengths):
-    gathered = lax.all_gather(tokens, "tensor", axis=0, tiled=True)
+    gathered = jnp.concatenate(
+        lax.all_to_all(jnp.stack([tokens] * lax.axis_size("tensor")), "tensor", 0, 0), axis=0
+    )
     count = gathered.shape[0]
     first = lax.axis_index("dp") * count
     positions = first + jnp.arange(count, dtype=jnp.int32)

time: 202 us -> 215 us (1.064)
  waiting for transfers between devices: 94.5 us -> 105 us
  matrix products: 18.3 us -> 14.5 us
  other arithmetic: 13.2 us -> 16.3 us
  starting transfers between devices: 33.3 us -> 35.5 us
    all_to_all x0 -> x1, waiting for transfers between devices: none -> 39.3 us  [body(): lax.all_to_all(jnp.stack([tokens] * lax.axis_size('tensor')), 'tensor', 0...]
    all_gather x1 -> x0, waiting for transfers between devices: 31.8 us -> none  [body(): gathered = lax.all_gather(tokens, 'tensor', axis=0, tiled=True)]
    convert_element_type x0 -> x2, other arithmetic: none -> 7.8 us  [project(): normed = (wide * inverse * norm_gain[None, :]).astype(jnp.bfloat16)]
    ppermute x5, waiting for transfers between devices: 4.62 us -> 11.3 us  [from_behind(): return lax.ppermute(block, axis, route)]
    dot_general x0 -> x1, local copies, waits for them, and re-layouts: none -> 6.39 us  [project(): jnp.dot(normed, w_query, preferred_element_type=jnp.float32)]
    all_to_all x0 -> x1, starting transfers between devices: none -> 4.97 us  [body(): lax.all_to_all(jnp.stack([tokens] * lax.axis_size('tensor')), 'tensor', 0...]
    another operation x0 -> x1, local copies, waits for them, and re-layouts: none -> 3.79 us  [body(): jnp.stack([tokens] * lax.axis_size('tensor'))]
    slice x6, local copies, waits for them, and re-layouts: 7.09 us -> 3.42 us  [attend_block(): positions[-1]]
  transfers between devices with their start and end apart: 7 -> 7, of which waited for: 7 -> 7; matrix products, arithmetic and copies ran while one was open for 9% -> 6% of each run, Pallas kernels for 0% -> 0%
where the time goes in v1:
time: 215 us; the launch traced here: 214 us
  waiting for transfers between devices  105 us (49%)
  starting transfers between devices  35.5 us (17%)
  local copies, waits for them, and re-layouts  21.8 us (10%)
  other arithmetic  16.3 us (8%)
  between operations  14.8 us (7%)
  matrix products  14.5 us (7%)
  loops' own time  6.27 us (3%)
    reduce_scatter x1, waiting for transfers between devices, body(): lax.psum_scatter(jnp.dot(attended, w_out, preferred_element_type=jnp.floa...  54.5 us
    all_to_all x1, waiting for transfers between devices, body(): lax.all_to_all(jnp.stack([tokens] * lax.axis_size('tensor')), 'tensor', 0...  39.3 us
    ppermute x5, starting transfers between devices, from_behind(): return lax.ppermute(block, axis, route)  30.5 us
    ppermute x5, waiting for transfers between devices, from_behind(): return lax.ppermute(block, axis, route)  11.3 us
    convert_element_type x2, other arithmetic, project(): normed = (wide * inverse * norm_gain[None, :]).astype(jnp.bfloat16)  7.8 us
    dot_general x1, matrix products, body(): jnp.dot(attended, w_out, preferred_element_type=jnp.float32)  6.5 us
    dot_general x1, local copies, waits for them, and re-layouts, project(): jnp.dot(normed, w_query, preferred_element_type=jnp.float32)  6.39 us
    another operation x1, loops' own time, body(): paired, carry = lax.fori_loop(1, reach + 1, one_step, (paired, carry))  6.03 us
  transfers between devices with their start and end apart: 7, of which 7 were waited for; matrix products, arithmetic and copies ran while one was open for 6% of the time, Pallas kernels for 0%

profile of v1, /device:TPU:0, one launch (start us, length us, event | category | flops | bytes accessed | tf_op | source)
XLA Modules:
  0.0 214.2 jit_solution(3879692780226005350)
XLA Ops:
  6.5 3.8 %stack.6 = bf16[4,128,4096]{2,1,0:T(8,128)(2,1)} broadcast(bf16[128,4096]{1,0:T(8,128)(2,1)} %param.13), dimensions={1,2} | broadcast | bytes 5242880 | tf_op jit(solution)/shard_map/stack | solution.py:113
  10.3 5.0 %all-to-all-start = ((bf16[4,128,4096]{2,1,0:T(8,128)(2,1)}), bf16[4,128,4096]{2,1,0:T(8,128)(2,1)}, u32[]{:S(2)}, u32[]{:S(2)}) async-start(bf16[4,128,4096]{2,1,0:T(8,128)(2,1)} %stack.6), calls=%async_computation | async-start | bytes 8388608 | tf_op jit(solution)/shard_map/all_to_all | solution.py:113
  15.4 0.5 slice.69
  16.2 0.5 slice.68
  17.9 6.4 %copy.42 = bf16[512,4096]{1,0:T(8,128)(2,1)} copy(bf16[512,4096]{0,1:T(8,128)(2,1)} %bitcast.154) | data formatting | bytes 8388608 | tf_op jit(solution)/shard_map/dot_general | solution.py:46
  24.4 0.5 multiply_cosine_fusion
  25.0 39.3 %all-to-all-done = bf16[4,128,4096]{2,1,0:T(8,128)(2,1)} async-done(((bf16[4,128,4096]{2,1,0:T(8,128)(2,1)}), bf16[4,128,4096]{2,1,0:T(8,128)(2,1)}, u32[]{:S(2)}, u32[]{:S(2)}) %all-to-all-start) | async-done | bytes 4194336 | tf_op jit(solution)/shard_map/all_to_all | solution.py:113
  64.2 3.1 %multiply_reduce_fusion = f32[4,128]{1,0:T(4,128)S(1)} fusion(bf16[4,128,4096]{2,1,0:T(8,128)(2,1)} %all-to-all-done), kind=kLoop, calls=%fused_computation.49 | loop fusion | flops 6290944 | bytes 4196352 | tf_op jit(solution)/shard_map/reduce_sum | solution.py:43
  67.3 3.8 %fusion.43 = bf16[512,4096]{1,0:T(8,128)(2,1)S(1)} fusion(bf16[4,128,4096]{2,1,0:T(8,128)(2,1)} %all-to-all-done, f32[4096]{0:T(1024)S(1)} %copy-done.4, f32[512]{0:T(512)S(1)} %get-tuple-element.568), kind=kLoop, calls=%fused_computation.47 | loop fusion | flops 8388608 | bytes 8407040 | tf_op jit(solution)/shard_map/convert_element_type | solution.py:44
  71.2 1.5 convolution_convert_fusion.1
  72.7 1.5 convolution_bitcast_fusion
  74.3 0.6 fusion.51
  74.9 0.8 copy.34
  75.7 4.0 %multiply_convert_fusion = bf16[4,128,4096]{2,1,0:T(8,128)(2,1)S(1)} fusion(bf16[4,128,4096]{2,1,0:T(8,128)(2,1)} %all-to-all-done, f32[4096]{0:T(1024)S(1)} %copy-done.4, f32[4,128]{1,0:T(4,128)S(1)} %get-tuple-element.567), kind=kLoop, calls=%fused_computation.48 | loop fusion | flops 8388608 | bytes 8407040 | tf_op jit(solution)/shard_map/convert_element_type | solution.py:44
  79.7 2.4 %fusion.55 = f32[512,4,128]{0,2,1:T(8,128)S(1)} fusion(bf16[512,4096,1]{1,0,2:T(8,128)(2,1)S(1)} %bitcast.153, bf16[4,128,4096]{2,1,0:T(8,128)(2,1)S(1)} %bitcast.155), kind=kOutput, calls=%fused_computation.80 | convolution fusion | flops 2147483648 | bytes 9437184 | tf_op jit(solution)/shard_map/dot_general | solution.py:46
  82.6 4.0 %conditional.2 = ((f32[512,1,4]{0,2,1:T(4,128)S(1)}, f32[512,1,4]{0,2,1:T(4,128)S(1)}, f32[512,1,4,128]{3,0,2,1:T(8,128)S(1)})) conditional(s32[]{:T(128)} %convert_element_type.103, (f32[512,1,4]{0,2,1:T(4,128)S(1)}, f32[512,1,4]{0,2,1:T(4,128)S(1)}, f32[512,1,4,128]{3,0,2,1:T(8,128)S(1)}) %tuple.55, (s32[512]{0:T(512)S(1)}, s32[512]{0:T(512)S(1)}, ...), branch_computations={%region_3.4_spmd, %region_4.7_spmd} | conditional | flops 549722112 | bytes 16650272 | solution.py:94
  83.1 0.9 fusion.2
  84.0 0.9 fusion.1
  84.9 1.6 fusion.10
  86.6 56.9 %while.45 = (s32[]{:T(128)}, bf16[2,512,128]{2,1,0:T(8,128)(2,1)}, f32[512,1,4]{0,2,1:T(4,128)S(1)}, f32[512,1,4]{0,2,1:T(4,128)S(1)}, f32[512,1,4,128]{3,0,2,1:...) while((s32[]{:T(128)}, bf16[2,512,128]{2,1,0:T(8,128)(2,1)}, ...), condition=%wide.region_12.13_spmd, body=%wide.region_7.12_spmd.sunk | while | flops 549722624 | bytes 18231664 | solution.py:141
  86.6 4.2 %collective-permute-start = (bf16[2,512,128]{2,1,0:T(8,128)(2,1)}, bf16[2,512,128]{2,1,0:T(8,128)(2,1)S(1)}, u32[]{:S(2)}, u32[]{:S(2)}) collective-permute-start(bf16[2,512,128]{2,1,0:T(8,128)(2,1)} %get-tuple-element.655), channel_id=1, source_target_pairs={{0,4},{4,8},{8,12},{12,16},{16,20},{20,24},{24,28},{1,5},{5,9},{9,... | collective-permute-start | bytes 786440 | tf_op jit(solution)/shard_map/while/body/eval_jaxpr/ppermute | solution.py:16
  90.8 0.5 slice.104
  91.3 0.6 slice.105
  93.0 3.3 %collective-permute-done = bf16[2,512,128]{2,1,0:T(8,128)(2,1)S(1)} collective-permute-done((bf16[2,512,128]{2,1,0:T(8,128)(2,1)}, bf16[2,512,128]{2,1,0:T(8,128)(2,1)S(1)}, u32[]{:S(2)}, u32[]{:S(2)}) %collective-permute-start) | collective-permute-done | bytes 262176 | tf_op jit(solution)/shard_map/while/body/eval_jaxpr/ppermute | solution.py:16
  96.3 0.7 copy.66
  97.0 8.0 %collective-permute-start = (bf16[2,512,128]{2,1,0:T(8,128)(2,1)}, bf16[2,512,128]{2,1,0:T(8,128)(2,1)S(1)}, u32[]{:S(2)}, u32[]{:S(2)}) collective-permute-start(bf16[2,512,128]{2,1,0:T(8,128)(2,1)} %get-tuple-element.655), channel_id=1, source_target_pairs={{0,4},{4,8},{8,12},{12,16},{16,20},{20,24},{24,28},{1,5},{5,9},{9,... | collective-permute-start | bytes 786440 | tf_op jit(solution)/shard_map/while/body/eval_jaxpr/ppermute | solution.py:16
  105.0 0.5 slice.104
  105.5 0.6 slice.105
  107.3 2.4 %collective-permute-done = bf16[2,512,128]{2,1,0:T(8,128)(2,1)S(1)} collective-permute-done((bf16[2,512,128]{2,1,0:T(8,128)(2,1)}, bf16[2,512,128]{2,1,0:T(8,128)(2,1)S(1)}, u32[]{:S(2)}, u32[]{:S(2)}) %collective-permute-start) | collective-permute-done | bytes 262176 | tf_op jit(solution)/shard_map/while/body/eval_jaxpr/ppermute | solution.py:16
  109.7 0.7 copy.66
  110.4 4.4 %collective-permute-start = (bf16[2,512,128]{2,1,0:T(8,128)(2,1)}, bf16[2,512,128]{2,1,0:T(8,128)(2,1)S(1)}, u32[]{:S(2)}, u32[]{:S(2)}) collective-permute-start(bf16[2,512,128]{2,1,0:T(8,128)(2,1)} %get-tuple-element.655), channel_id=1, source_target_pairs={{0,4},{4,8},{8,12},{12,16},{16,20},{20,24},{24,28},{1,5},{5,9},{9,... | collective-permute-start | bytes 786440 | tf_op jit(solution)/shard_map/while/body/eval_jaxpr/ppermute | solution.py:16
  114.7 0.5 slice.104
  115.3 0.6 slice.105
  117.0 1.9 collective-permute-done
  118.9 0.7 copy.66
  119.6 8.8 %collective-permute-start = (bf16[2,512,128]{2,1,0:T(8,128)(2,1)}, bf16[2,512,128]{2,1,0:T(8,128)(2,1)S(1)}, u32[]{:S(2)}, u32[]{:S(2)}) collective-permute-start(bf16[2,512,128]{2,1,0:T(8,128)(2,1)} %get-tuple-element.655), channel_id=1, source_target_pairs={{0,4},{4,8},{8,12},{12,16},{16,20},{20,24},{24,28},{1,5},{5,9},{9,... | collective-permute-start | bytes 786440 | tf_op jit(solution)/shard_map/while/body/eval_jaxpr/ppermute | solution.py:16
  128.5 0.5 slice.104
  129.0 0.6 slice.105
  130.8 1.9 collective-permute-done
  132.7 0.7 copy.66
  133.4 5.2 %collective-permute-start = (bf16[2,512,128]{2,1,0:T(8,128)(2,1)}, bf16[2,512,128]{2,1,0:T(8,128)(2,1)S(1)}, u32[]{:S(2)}, u32[]{:S(2)}) collective-permute-start(bf16[2,512,128]{2,1,0:T(8,128)(2,1)} %get-tuple-element.655), channel_id=1, source_target_pairs={{0,4},{4,8},{8,12},{12,16},{16,20},{20,24},{24,28},{1,5},{5,9},{9,... | collective-permute-start | bytes 786440 | tf_op jit(solution)/shard_map/while/body/eval_jaxpr/ppermute | solution.py:16
  138.6 0.5 slice.104
  139.1 0.6 slice.105
  140.8 1.9 collective-permute-done
  142.7 0.7 copy.66
  143.9 6.5 %convolution_convert_fusion = bf16[512,4096]{1,0:T(8,128)(2,1)} fusion(bf16[512,512]{0,1:T(8,128)(2,1)S(1)} %bitcast.158, bf16[512,4096]{1,0:T(8,128)(2,1)} %param.18), kind=kOutput, calls=%fused_computation.50 | convolution fusion | flops 2149580800 | bytes 8912896 | tf_op jit(solution)/shard_map/dot_general | solution.py:145
  150.4 54.5 %reduce-scatter.2.cloned.1.call-done = bf16[128,4096]{1,0:T(8,128)(2,1)} async-done(((bf16[512,4096]{1,0:T(8,128)(2,1)}), bf16[128,4096]{1,0:T(8,128)(2,1)}) %reduce-scatter.2.cloned.1.call-update) | async-done | bytes 1048592 | tf_op jit(solution)/shard_map/reduce_scatter | solution.py:144
  204.9 2.4 %add_convert_fusion = bf16[128,4096]{1,0:T(8,128)(2,1)} fusion(bf16[128,4096]{1,0:T(8,128)(2,1)} %reduce-scatter.2.cloned.1.call-done, bf16[128,4096]{1,0:T(8,128)(2,1)S(1)} %copy-done.1), kind=kLoop, calls=%fused_computation.51 | loop fusion | flops 2097152 | bytes 3145728 | tf_op jit(solution)/shard_map/convert_element_type | solution.py:150
  (44 shorter events, 1.7 us)
Async XLA Ops:
  6.5 64.6 %copy-start = (bf16[4096,128]{1,0:T(8,128)(2,1)S(1)}, bf16[4096,128]{1,0:T(8,128)(2,1)}, u32[]{:S(2)}) copy-start(bf16[4096,128]{1,0:T(8,128)(2,1)} %param.17) | copy-start | bytes 3145732
  10.3 5.6 %copy-start.5 = (s32[4]{0:T(128)S(1)}, s32[4]{0:T(128)}, u32[]{:S(2)}) copy-start(s32[4]{0:T(128)} %param.19) | copy-start | bytes 52
  10.3 53.9 %all-to-all-start = ((bf16[4,128,4096]{2,1,0:T(8,128)(2,1)}), bf16[4,128,4096]{2,1,0:T(8,128)(2,1)}, u32[]{:S(2)}, u32[]{:S(2)}) async-start(bf16[4,128,4096]{2,1,0:T(8,128)(2,1)} %stack.6), calls=%async_computation | async-start | bytes 8388608 | tf_op jit(solution)/shard_map/all_to_all | solution.py:113
  15.3 189.6 %reduce-scatter.2.cloned.1.call-start = ((), (), s32[]{:S(2)}) async-start(), calls=%async_computation.2 | async-start | bytes 5242880 | tf_op jit(solution)/shard_map/reduce_scatter | solution.py:144
  24.3 43.0 %copy-start.4 = (f32[4096]{0:T(1024)S(1)}, f32[4096]{0:T(1024)}, u32[]{:S(2)}) copy-start(f32[4096]{0:T(1024)} %param.14) | copy-start | bytes 49156
  71.2 1.6 copy-start.3
  75.7 4.0 %copy-start.2 = (bf16[512,4096]{1,0:T(8,128)(2,1)S(1)}, bf16[512,4096]{1,0:T(8,128)(2,1)}, u32[]{:S(2)}) copy-start(bf16[512,4096]{1,0:T(8,128)(2,1)} %copy.42) | copy-start | bytes 12582916
  86.6 9.7 %collective-permute-start = (bf16[2,512,128]{2,1,0:T(8,128)(2,1)}, bf16[2,512,128]{2,1,0:T(8,128)(2,1)S(1)}, u32[]{:S(2)}, u32[]{:S(2)}) collective-permute-start(bf16[2,512,128]{2,1,0:T(8,128)(2,1)} %get-tuple-element.655), channel_id=1, source_target_pairs={{0,4},{4,8},{8,12},{12,16},{16,20},{20,24},{24,28},{1,5},{5,9},{9,... | collective-permute-start | bytes 786440 | tf_op jit(solution)/shard_map/while/body/eval_jaxpr/ppermute | solution.py:16
  97.0 12.7 %collective-permute-start = (bf16[2,512,128]{2,1,0:T(8,128)(2,1)}, bf16[2,512,128]{2,1,0:T(8,128)(2,1)S(1)}, u32[]{:S(2)}, u32[]{:S(2)}) collective-permute-start(bf16[2,512,128]{2,1,0:T(8,128)(2,1)} %get-tuple-element.655), channel_id=1, source_target_pairs={{0,4},{4,8},{8,12},{12,16},{16,20},{20,24},{24,28},{1,5},{5,9},{9,... | collective-permute-start | bytes 786440 | tf_op jit(solution)/shard_map/while/body/eval_jaxpr/ppermute | solution.py:16
  110.4 8.5 %collective-permute-start = (bf16[2,512,128]{2,1,0:T(8,128)(2,1)}, bf16[2,512,128]{2,1,0:T(8,128)(2,1)S(1)}, u32[]{:S(2)}, u32[]{:S(2)}) collective-permute-start(bf16[2,512,128]{2,1,0:T(8,128)(2,1)} %get-tuple-element.655), channel_id=1, source_target_pairs={{0,4},{4,8},{8,12},{12,16},{16,20},{20,24},{24,28},{1,5},{5,9},{9,... | collective-permute-start | bytes 786440 | tf_op jit(solution)/shard_map/while/body/eval_jaxpr/ppermute | solution.py:16
  119.6 13.0 %collective-permute-start = (bf16[2,512,128]{2,1,0:T(8,128)(2,1)}, bf16[2,512,128]{2,1,0:T(8,128)(2,1)S(1)}, u32[]{:S(2)}, u32[]{:S(2)}) collective-permute-start(bf16[2,512,128]{2,1,0:T(8,128)(2,1)} %get-tuple-element.655), channel_id=1, source_target_pairs={{0,4},{4,8},{8,12},{12,16},{16,20},{20,24},{24,28},{1,5},{5,9},{9,... | collective-permute-start | bytes 786440 | tf_op jit(solution)/shard_map/while/body/eval_jaxpr/ppermute | solution.py:16
  133.4 9.4 %collective-permute-start = (bf16[2,512,128]{2,1,0:T(8,128)(2,1)}, bf16[2,512,128]{2,1,0:T(8,128)(2,1)S(1)}, u32[]{:S(2)}, u32[]{:S(2)}) collective-permute-start(bf16[2,512,128]{2,1,0:T(8,128)(2,1)} %get-tuple-element.655), channel_id=1, source_target_pairs={{0,4},{4,8},{8,12},{12,16},{16,20},{20,24},{24,28},{1,5},{5,9},{9,... | collective-permute-start | bytes 786440 | tf_op jit(solution)/shard_map/while/body/eval_jaxpr/ppermute | solution.py:16
  150.4 54.5 %copy-start.1 = (bf16[128,4096]{1,0:T(8,128)(2,1)S(1)}, bf16[128,4096]{1,0:T(8,128)(2,1)}, u32[]{:S(2)}) copy-start(bf16[128,4096]{1,0:T(8,128)(2,1)} %param.13) | copy-start | bytes 3145732
Sparse Core Ops, SparseCore 0:
  150.6 54.3 reduce-scatter.1
